TPU v7x, 32 devices: a whole 2x2x4 slice. The times are simulated.
32 devices in a mesh: kpt: 2 (over core), orb: 16 (over z, y, x).
Axes of the slice: x: 2, y: 2, z: 4, core: 2. Of those that a mesh axis runs over, the one named last changes fastest.
Arguments:
- orbitals: bfloat16 [2, 512, 64, 1024], P('kpt', 'orb'), may hold values from -6 to 6
- potential: float32 [64, 1024], replicated, may hold values from 0.5 to 12
Outputs:
- rotated: bfloat16 [2, 512, 64, 1024], P('kpt', 'orb')
- density: float32 [64, 1024], P('orb')
All inputs are finite; a program needn't handle non-finite values.
Results may differ from a plain program's by a relative error of at most 0.0068.
The roundings to bfloat16 on the way count: a program that leaves them out, or rounds other values in their place, can miss the bound.
Values may be sent and summed in bfloat16 or wider, within the bound.
No kernel may reach another device: no remote copies, remote signals or barrier semaphores. Data moves between devices by JAX's collectives and lax.ppermute only.
A program may use at most 128 MiB of HBM per device.

v0:
```python
import math
import jax
import jax.numpy as jnp
import numpy as np
from jax import lax
from jax.sharding import PartitionSpec as P

NX = 64
NY = 32
NZ = 32
DEG = 4
ITERS = 8
filter_centre = 13.0
filter_half = 9.0
margin_eps = 1e-06


def circulant(taps, first, length):
    matrix = np.zeros((length, length))
    for k in range(len(taps)):
        for i in range(length):
            matrix[i, (i + first + k) % length] += taps[k]
    return matrix


def build_tables(size_x, size_y, size_z):
    kinetic = [math.pi**2 / 6.0 if k == 0 else (-1.0) ** k / (k * k) for k in range(-14, 15)]
    smooth_taps = np.array([math.exp(-((k + 0.5) ** 2) / 6.0) for k in range(-8, 8)])
    smooth_taps = smooth_taps / smooth_taps.sum()
    kin_x = circulant(kinetic, -14, size_x)
    mag_x = circulant(smooth_taps, -8, size_x)
    kin_yz = np.kron(circulant(kinetic, -14, size_y), np.eye(size_z)) + np.kron(
        np.eye(size_y), circulant(kinetic, -14, size_z)
    )
    mag_yz = np.kron(circulant(smooth_taps, -8, size_y), circulant(smooth_taps, -8, size_z))
    yz_table = np.concatenate([kin_yz.T, mag_yz.T], axis=1)
    result = [kin_x, mag_x, mag_x.T, yz_table, mag_yz]
    return [jnp.asarray(table, jnp.float32).astype(jnp.bfloat16) for table in result]


def hamiltonian(block, potential, tables):
    kin_x, mag_x, mag_xt, yz_table, mag_yz = tables
    width = block.shape[2]
    both = jnp.einsum("bxc,cd->bxd", block, yz_table, preferred_element_type=jnp.float32)
    smooth = both[:, :, width:].astype(jnp.bfloat16)
    kin_all = (
        jnp.einsum("ux,bxc->buc", kin_x, block, preferred_element_type=jnp.float32)
        + both[:, :, :width]
    )
    weighted = (
        potential[None]
        * jnp.einsum("ux,bxc->buc", mag_x, smooth, preferred_element_type=jnp.float32)
    ).astype(jnp.bfloat16)
    back = jnp.einsum("ux,bxc->buc", mag_xt, weighted, preferred_element_type=jnp.float32).astype(
        jnp.bfloat16
    )
    return kin_all + jnp.einsum("bxc,cd->bxd", back, mag_yz, preferred_element_type=jnp.float32)


def chebyshev(block, potential, tables):
    prev = block
    shifted = hamiltonian(block, potential, tables) - filter_centre * block.astype(jnp.float32)
    now = (shifted / filter_half).astype(jnp.bfloat16)
    for step in range(DEG - 1):
        shifted = hamiltonian(now, potential, tables) - filter_centre * now.astype(jnp.float32)
        nxt = (2.0 * shifted / filter_half - prev.astype(jnp.float32)).astype(jnp.bfloat16)
        prev, now = (now, nxt)
    return now


def shards(orbitals, potential):
    width = orbitals.shape[3]
    tables = build_tables(NX, NY, NZ)
    hp = lax.Precision.HIGHEST
    filtered = chebyshev(orbitals[0], potential, tables)[None]
    spread = lax.all_to_all(filtered, "orb", split_axis=2, concat_axis=1, tiled=True)
    count_orb = spread.shape[1]
    rows_dev = spread.shape[2]
    cells = NX * NY * NZ
    flat = spread[0].reshape(count_orb, rows_dev * width)
    inverse_cells = 1.0 / cells
    partial_margin = (
        lax.dot_general(flat, flat, (((1,), (1,)), ((), ())), preferred_element_type=jnp.float32)
        * inverse_cells
    )
    margin = lax.psum(partial_margin, "orb")
    scale = jnp.sqrt(jnp.sum(margin * margin) + margin_eps)
    eye = jnp.eye(count_orb, dtype=jnp.float32)
    iterate_a = margin / scale
    iterate_z = eye
    for step in range(ITERS):
        factor = 0.5 * (3.0 * eye - jnp.dot(iterate_z, iterate_a, precision=hp))
        iterate_a = jnp.dot(factor, iterate_a, precision=hp)
        iterate_z = jnp.dot(factor, iterate_z, precision=hp)
    coeff = (iterate_z / jnp.sqrt(scale)).astype(jnp.bfloat16)
    rotated_flat = lax.dot_general(
        coeff, flat, (((0,), (0,)), ((), ())), preferred_element_type=jnp.float32
    ).astype(jnp.bfloat16)
    rotated_cells = rotated_flat.reshape(1, count_orb, rows_dev, width)
    rotated = lax.all_to_all(rotated_cells, "orb", split_axis=1, concat_axis=2, tiled=True)
    weight = 1.0 / (lax.axis_size("kpt") * math.sqrt(count_orb))
    values = rotated_flat.astype(jnp.float32)
    own_density = (jnp.sum(values * values, axis=0) * weight).reshape(rows_dev, width)
    density = lax.psum(own_density, "kpt")
    return (rotated, density)


def solution(mesh):
    in_specs = (P("kpt", "orb", None, None), P())
    out_specs = (P("kpt", "orb", None, None), P("orb", None))
    return jax.shard_map(shards, mesh=mesh, in_specs=in_specs, out_specs=out_specs, check_vma=False)
```

profile of v0, /device:TPU:14, one launch (start us, length us, event | category | flops | bytes accessed | tf_op | source)
XLA Modules:
  0.0 567.5 jit_solution(11716203920185398709)
XLA Ops:
  7.2 0.0 copy-start.14
  7.2 0.0 copy-start.15
  7.2 0.0 all-reduce.2.cloned.1.call-start
  7.2 15.1 %convolution_bitcast_fusion = f32[32,64,2048]{2,1,0:T(8,128)} fusion(bf16[1024,2048,1]{1,0,2:T(8,128)(2,1)} %constant.48, bf16[1,32,64,1024]{3,2,1,0:T(8,128)(2,1)} %param.7), kind=kOutput, calls=%fused_computation.39 | convolution fusion | flops 8589934592 | bytes 25165824 | tf_op jit(solution)/shard_map/bxc,cd->bxd/dot_general | solution.py:44
  22.4 7.7 %fusion.20 = bf16[32,1024,64]{1,2,0:T(8,128)(2,1)} fusion(bf16[64,64,1]{1,0,2:T(8,128)(2,1)S(1)} %copy-done.14, f32[64,1024]{1,0:T(8,128)S(1)} %copy-done.10, bf16[64,64,1]{1,0,2:T(8,128)(2,1)S(1)} %copy-done.15, f32[32,64,2048]{2,1,0:T(8,128)} %convolution_bitcast_fusion), kind=kOutput, calls=%fused_computation.41 | convolution fusion | flops 541065216 | bytes 8667136 | tf_op jit(solution)/shard_map/ux,bxc->buc/dot_general | solution.py:54
  30.1 7.1 %fusion.39 = f32[32,64,1024]{2,1,0:T(8,128)S(1)} fusion(bf16[1024,1024,1]{1,0,2:T(8,128)(2,1)} %constant.51, bf16[32,1024,64]{1,2,0:T(8,128)(2,1)} %fusion.20), kind=kOutput, calls=%fused_computation.56 | convolution fusion | flops 4294967296 | bytes 14680064 | tf_op jit(solution)/shard_map/bxc,cd->bxd/dot_general | solution.py:57
  37.2 5.4 fusion.2
  42.6 2.0 copy-done.3
  44.6 14.5 %fusion.65 = f32[32,64,2048]{2,1,0:T(8,128)} fusion(bf16[32,64,1024]{2,1,0:T(8,128)(2,1)S(1)} %fusion.2, bf16[1024,2048,1]{1,0,2:T(8,128)(2,1)} %constant.48), kind=kOutput, calls=%fused_computation.94 | convolution fusion | flops 8589934592 | bytes 25165824 | tf_op jit(solution)/shard_map/bxc,cd->bxd/dot_general | solution.py:44
  59.1 7.7 %fusion.22 = bf16[32,1024,64]{1,2,0:T(8,128)(2,1)} fusion(bf16[64,64,1]{1,0,2:T(8,128)(2,1)S(1)} %copy-done.14, f32[64,1024]{1,0:T(8,128)S(1)} %copy-done.10, bf16[64,64,1]{1,0,2:T(8,128)(2,1)S(1)} %copy-done.15, f32[32,64,2048]{2,1,0:T(8,128)} %fusion.65), kind=kOutput, calls=%fused_computation.42 | convolution fusion | flops 541065216 | bytes 8667136 | tf_op jit(solution)/shard_map/ux,bxc->buc/dot_general | solution.py:54
  66.8 10.8 %fusion.37 = f32[32,64,1024]{2,1,0:T(8,128)} fusion(bf16[1024,1024,1]{1,0,2:T(8,128)(2,1)} %constant.51, bf16[32,1024,64]{1,2,0:T(8,128)(2,1)} %fusion.22), kind=kOutput, calls=%fused_computation.54 | convolution fusion | flops 4294967296 | bytes 14680064 | tf_op jit(solution)/shard_map/bxc,cd->bxd/dot_general | solution.py:57
  77.5 7.6 %fusion.3 = bf16[32,64,1024]{2,1,0:T(8,128)(2,1)S(1)} fusion(bf16[32,64,1024]{2,1,0:T(8,128)(2,1)S(1)} %copy-done.4, f32[32,64,1024]{2,1,0:T(8,128)} %fusion.37, f32[32,64,2048]{2,1,0:T(8,128)} %fusion.65, bf16[1,32,64,1024]{3,2,1,0:T(8,128)(2,1)S(1)} %copy-done.9, bf16[64,64,1]{1,0,2:T(8,128)(2,1)S(1)} %copy-done.16), kind=kOutput, calls=%fused_computation.9 | convolution fusion | flops 287309824 | bytes 33570816 | tf_op jit(solution)/shard_map/ux,bxc->buc/dot_general | solution.py:47
  85.2 2.0 copy-done
  87.1 14.0 %fusion.66 = f32[32,64,2048]{2,1,0:T(8,128)} fusion(bf16[32,64,1024]{2,1,0:T(8,128)(2,1)S(1)} %fusion.3, bf16[1024,2048,1]{1,0,2:T(8,128)(2,1)} %constant.48), kind=kOutput, calls=%fused_computation.95 | convolution fusion | flops 8589934592 | bytes 25165824 | tf_op jit(solution)/shard_map/bxc,cd->bxd/dot_general | solution.py:44
  101.1 7.8 %fusion.24 = bf16[32,1024,64]{1,2,0:T(8,128)(2,1)} fusion(bf16[64,64,1]{1,0,2:T(8,128)(2,1)S(1)} %copy-done.14, f32[64,1024]{1,0:T(8,128)S(1)} %copy-done.10, bf16[64,64,1]{1,0,2:T(8,128)(2,1)S(1)} %copy-done.15, f32[32,64,2048]{2,1,0:T(8,128)} %fusion.66), kind=kOutput, calls=%fused_computation.43 | convolution fusion | flops 541065216 | bytes 8667136 | tf_op jit(solution)/shard_map/ux,bxc->buc/dot_general | solution.py:54
  108.9 9.2 %fusion.35 = f32[32,64,1024]{2,1,0:T(8,128)} fusion(bf16[1024,1024,1]{1,0,2:T(8,128)(2,1)S(1)} %copy-done.17, bf16[32,1024,64]{1,2,0:T(8,128)(2,1)} %fusion.24), kind=kOutput, calls=%fused_computation.52 | convolution fusion | flops 4294967296 | bytes 14680064 | tf_op jit(solution)/shard_map/bxc,cd->bxd/dot_general | solution.py:57
  118.1 7.6 %fusion.6 = bf16[32,64,1024]{2,1,0:T(8,128)(2,1)S(1)} fusion(bf16[32,64,1024]{2,1,0:T(8,128)(2,1)S(1)} %copy-done.5, bf16[32,64,1024]{2,1,0:T(8,128)(2,1)S(1)} %copy-done.1, f32[32,64,1024]{2,1,0:T(8,128)} %fusion.35, f32[32,64,2048]{2,1,0:T(8,128)} %fusion.66, bf16[64,64,1]{1,0,2:T(8,128)(2,1)S(1)} %copy-done.16), kind=kOutput, calls=%fused_computation.12 | convolution fusion | flops 287309824 | bytes 33570816 | tf_op jit(solution)/shard_map/ux,bxc->buc/dot_general | solution.py:47
  125.7 0.0 copy-start.6
  125.8 2.0 copy-done.6
  127.8 14.1 %fusion.67 = f32[32,64,2048]{2,1,0:T(8,128)} fusion(bf16[32,64,1024]{2,1,0:T(8,128)(2,1)S(1)} %fusion.6, bf16[1024,2048,1]{1,0,2:T(8,128)(2,1)} %constant.48), kind=kOutput, calls=%fused_computation.96 | convolution fusion | flops 8589934592 | bytes 25165824 | tf_op jit(solution)/shard_map/bxc,cd->bxd/dot_general | solution.py:44
  141.8 7.8 %fusion.26 = bf16[32,1024,64]{1,2,0:T(8,128)(2,1)} fusion(bf16[64,64,1]{1,0,2:T(8,128)(2,1)S(1)} %copy-done.14, f32[64,1024]{1,0:T(8,128)S(1)} %copy-done.10, bf16[64,64,1]{1,0,2:T(8,128)(2,1)S(1)} %copy-done.15, f32[32,64,2048]{2,1,0:T(8,128)} %fusion.67), kind=kOutput, calls=%fused_computation.44 | convolution fusion | flops 541065216 | bytes 8667136 | tf_op jit(solution)/shard_map/ux,bxc->buc/dot_general | solution.py:54
  149.6 9.2 %fusion.33 = f32[32,64,1024]{2,1,0:T(8,128)} fusion(bf16[1024,1024,1]{1,0,2:T(8,128)(2,1)S(1)} %copy-done.18, bf16[32,1024,64]{1,2,0:T(8,128)(2,1)} %fusion.26), kind=kOutput, calls=%fused_computation.50 | convolution fusion | flops 4294967296 | bytes 14680064 | tf_op jit(solution)/shard_map/bxc,cd->bxd/dot_general | solution.py:57
  158.8 7.6 %fusion.32 = bf16[1,32,64,1024]{3,2,1,0:T(8,128)(2,1)S(1)} fusion(bf16[32,64,1024]{2,1,0:T(8,128)(2,1)S(1)} %copy-done.2, bf16[32,64,1024]{2,1,0:T(8,128)(2,1)S(1)} %copy-done.7, f32[32,64,1024]{2,1,0:T(8,128)} %fusion.33, f32[32,64,2048]{2,1,0:T(8,128)} %fusion.67, bf16[64,64,1]{1,0,2:T(8,128)(2,1)S(1)} %copy-done.16), kind=kOutput, calls=%fused_computation.49 | convolution fusion | flops 287309824 | bytes 33570816 | tf_op jit(solution)/shard_map/ux,bxc->buc/dot_general | solution.py:47
  166.4 2.3 copy.12
  168.8 98.6 %all_to_all.33 = bf16[1,32,64,1024]{3,1,0,2:T(8,128)(2,1)S(1)} all-to-all(bf16[1,32,64,1024]{3,1,0,2:T(8,128)(2,1)S(1)} %copy.12), channel_id=1, replica_groups=mesh['kpt'=2,'orb'=16] {'orb'}, dimensions={2} | all-to-all | bytes 8388608 | tf_op jit(solution)/shard_map/all_to_all | solution.py:76
  267.4 3.5 copy.13
  270.9 2.3 copy.16
  273.3 0.0 copy-start.11
  273.3 2.0 copy-done.11
  275.3 3.4 convolution_multiply_fusion
  278.6 0.0 all-reduce.2.cloned.1.call-update
  278.7 112.0 %all-reduce.2.cloned.1.call-done = f32[512,512]{1,0:T(8,128)} async-done(((f32[512,512]{1,0:T(8,128)}), f32[512,512]{1,0:T(8,128)}) %all-reduce.2.cloned.1.call-update) | async-done | bytes 1048592 | tf_op jit(solution)/shard_map/psum | solution.py:86
  390.6 2.2 multiply_reduce_fusion.1
  393.6 2.3 fusion.61
  395.9 1.0 fusion.63
  396.9 2.0 fusion.64
  398.9 1.8 fusion.54
  400.8 1.8 fusion.69
  402.6 1.8 fusion.68
  404.5 1.9 fusion.55
  406.4 1.8 fusion.71
  408.2 1.8 fusion.70
  410.1 2.1 fusion.56
  412.2 1.8 fusion.73
  414.0 1.8 fusion.72
  415.9 1.9 fusion.57
  417.7 1.8 fusion.75
  419.6 1.8 fusion.74
  421.4 1.8 fusion.58
  423.3 2.3 fusion.77
  425.6 1.8 fusion.76
  427.4 1.8 fusion.59
  429.3 1.8 fusion.78
  431.1 1.8 fusion.79
  433.0 0.0 copy-start.12
  433.0 1.8 fusion.60
  434.9 1.9 fusion.62
  436.7 4.6 multiply_reduce_fusion
  441.4 7.9 %reshape.13 = bf16[1,512,4,1024]{3,2,1,0:T(4,128)(2,1)} reshape(bf16[512,4096]{1,0:T(8,128)(2,1)} %get-tuple-element.3) | data formatting | bytes 8388608 | tf_op jit(solution)/shard_map/reshape | solution.py:99
  449.2 5.8 %all-to-all-start.1 = ((bf16[1,512,4,1024]{3,2,0,1:T(4,128)(2,1)}), bf16[1,512,4,1024]{3,2,0,1:T(4,128)(2,1)}, u32[]{:S(2)}, u32[]{:S(2)}) async-start(bf16[1,512,4,1024]{3,2,0,1:T(4,128)(2,1)} %bitcast.141), calls=%async_computation.1 | async-start | bytes 8388608 | tf_op jit(solution)/shard_map/all_to_all | solution.py:100
  455.0 4.0 psum.15
  459.0 88.2 %all-to-all-done.1 = bf16[1,512,4,1024]{3,2,0,1:T(4,128)(2,1)} async-done(((bf16[1,512,4,1024]{3,2,0,1:T(4,128)(2,1)}), bf16[1,512,4,1024]{3,2,0,1:T(4,128)(2,1)}, u32[]{:S(2)}, u32[]{:S(2)}) %all-to-all-start.1) | async-done | bytes 4194336 | tf_op jit(solution)/shard_map/all_to_all | solution.py:100
  547.2 6.4 %copy.15 = bf16[1,32,16,4,1024]{4,3,2,1,0:T(4,128)(2,1)} copy(bf16[1,32,16,4,1024]{4,3,1,2,0:T(4,128)(2,1)} %bitcast.24) | data formatting | bytes 8388608 | tf_op jit(solution)/shard_map/all_to_all | solution.py:100
  553.6 6.9 %all_to_all.30 = bf16[1,32,64,1024]{3,2,1,0:T(8,128)(2,1)} reshape(bf16[1,32,16,4,1024]{4,3,2,1,0:T(4,128)(2,1)} %copy.15) | data formatting | bytes 8388608 | tf_op jit(solution)/shard_map/all_to_all | solution.py:100
  (31 shorter events, 0.1 us)
Async XLA Ops:
  7.2 15.2 %copy-start.14 = (bf16[64,64,1]{1,0,2:T(8,128)(2,1)S(1)}, bf16[64,64,1]{1,0,2:T(8,128)(2,1)}, u32[]{:S(2)}) copy-start(bf16[64,64,1]{1,0,2:T(8,128)(2,1)} %constant.50) | copy-start | bytes 24580
  7.2 15.2 %copy-start.15 = (bf16[64,64,1]{1,0,2:T(8,128)(2,1)S(1)}, bf16[64,64,1]{1,0,2:T(8,128)(2,1)}, u32[]{:S(2)}) copy-start(bf16[64,64,1]{1,0,2:T(8,128)(2,1)} %constant.49) | copy-start | bytes 24580
  7.2 15.2 %copy-start.10 = (f32[64,1024]{1,0:T(8,128)S(1)}, f32[64,1024]{1,0:T(8,128)}, u32[]{:S(2)}) copy-start(f32[64,1024]{1,0:T(8,128)} %param.8) | copy-start | bytes 786436
  7.2 383.4 %all-reduce.2.cloned.1.call-start = ((), (), s32[]{:S(2)}) async-start(), calls=%async_computation.2 | async-start | bytes 2097152 | tf_op jit(solution)/shard_map/psum | solution.py:86
  30.1 7.1 %copy-start.8 = (bf16[1,32,64,1024]{3,2,1,0:T(8,128)(2,1)S(1)}, bf16[1,32,64,1024]{3,2,1,0:T(8,128)(2,1)}, u32[]{:S(2)}) copy-start(bf16[1,32,64,1024]{3,2,1,0:T(8,128)(2,1)} %param.7) | copy-start | bytes 12582916
  30.1 7.1 %copy-start.16 = (bf16[64,64,1]{1,0,2:T(8,128)(2,1)S(1)}, bf16[64,64,1]{1,0,2:T(8,128)(2,1)}, u32[]{:S(2)}) copy-start(bf16[64,64,1]{1,0,2:T(8,128)(2,1)} %constant.47) | copy-start | bytes 24580
  42.6 2.0 copy-start.3
  66.7 10.8 %copy-start.4 = (bf16[32,64,1024]{2,1,0:T(8,128)(2,1)S(1)}, bf16[32,64,1024]{2,1,0:T(8,128)(2,1)}, u32[]{:S(2)}) copy-start(bf16[32,64,1024]{2,1,0:T(8,128)(2,1)} %copy-done.3) | copy-start | bytes 12582916
  66.7 10.8 %copy-start.9 = (bf16[1,32,64,1024]{3,2,1,0:T(8,128)(2,1)S(1)}, bf16[1,32,64,1024]{3,2,1,0:T(8,128)(2,1)}, u32[]{:S(2)}) copy-start(bf16[1,32,64,1024]{3,2,1,0:T(8,128)(2,1)} %param.7) | copy-start | bytes 12582916
  85.1 2.0 copy-start
  101.1 7.8 %copy-start.17 = (bf16[1024,1024,1]{1,0,2:T(8,128)(2,1)S(1)}, bf16[1024,1024,1]{1,0,2:T(8,128)(2,1)}, u32[]{:S(2)}) copy-start(bf16[1024,1024,1]{1,0,2:T(8,128)(2,1)} %constant.51) | copy-start | bytes 6291460
  108.9 9.2 %copy-start.1 = (bf16[32,64,1024]{2,1,0:T(8,128)(2,1)S(1)}, bf16[32,64,1024]{2,1,0:T(8,128)(2,1)}, u32[]{:S(2)}) copy-start(bf16[32,64,1024]{2,1,0:T(8,128)(2,1)} %copy-done) | copy-start | bytes 12582916
  108.9 9.2 %copy-start.5 = (bf16[32,64,1024]{2,1,0:T(8,128)(2,1)S(1)}, bf16[32,64,1024]{2,1,0:T(8,128)(2,1)}, u32[]{:S(2)}) copy-start(bf16[32,64,1024]{2,1,0:T(8,128)(2,1)} %copy-done.3) | copy-start | bytes 12582916
  125.7 2.0 copy-start.6
  141.8 7.8 %copy-start.18 = (bf16[1024,1024,1]{1,0,2:T(8,128)(2,1)S(1)}, bf16[1024,1024,1]{1,0,2:T(8,128)(2,1)}, u32[]{:S(2)}) copy-start(bf16[1024,1024,1]{1,0,2:T(8,128)(2,1)} %constant.51) | copy-start | bytes 6291460
  149.6 9.2 %copy-start.2 = (bf16[32,64,1024]{2,1,0:T(8,128)(2,1)S(1)}, bf16[32,64,1024]{2,1,0:T(8,128)(2,1)}, u32[]{:S(2)}) copy-start(bf16[32,64,1024]{2,1,0:T(8,128)(2,1)} %copy-done) | copy-start | bytes 12582916
  149.6 9.2 %copy-start.7 = (bf16[32,64,1024]{2,1,0:T(8,128)(2,1)S(1)}, bf16[32,64,1024]{2,1,0:T(8,128)(2,1)}, u32[]{:S(2)}) copy-start(bf16[32,64,1024]{2,1,0:T(8,128)(2,1)} %copy-done.6) | copy-start | bytes 12582916
  273.3 2.0 copy-start.11
  390.6 6.2 %copy-start.13 = (f32[512,512]{1,0:T(8,128)S(1)}, f32[512,512]{1,0:T(8,128)}, u32[]{:S(2)}) copy-start(f32[512,512]{1,0:T(8,128)} %all-reduce.2.cloned.1.call-done) | copy-start | bytes 3145732
  433.0 3.7 copy-start.12
  449.2 97.9 %all-to-all-start.1 = ((bf16[1,512,4,1024]{3,2,0,1:T(4,128)(2,1)}), bf16[1,512,4,1024]{3,2,0,1:T(4,128)(2,1)}, u32[]{:S(2)}, u32[]{:S(2)}) async-start(bf16[1,512,4,1024]{3,2,0,1:T(4,128)(2,1)} %bitcast.141), calls=%async_computation.1 | async-start | bytes 8388608 | tf_op jit(solution)/shard_map/all_to_all | solution.py:100
Sparse Core Ops, SparseCore 0:
  278.8 111.7 all-reduce.1
where the time goes:
time: 575 us; the launch traced here: 567 us
  matrix products  204 us (35%)
  waiting for transfers between devices  200 us (35%)
  blocking collectives  103 us (18%)
  local copies, waits for them, and re-layouts  37.4 us (7%)
  between operations  15.3 us (3%)
  starting transfers between devices  5.82 us (1%)
    psum x1, waiting for transfers between devices, shards(): margin = lax.psum(partial_margin, 'orb')  112 us
    all_to_all x1, blocking collectives, shards(): lax.all_to_all(filtered, 'orb', split_axis=2, concat_axis=1, tiled=True)  98.6 us
    all_to_all x1, waiting for transfers between devices, shards(): lax.all_to_all(rotated_cells, 'orb', split_axis=1, concat_axis=2, tiled=T...  88.2 us
    dot_general x4, matrix products, hamiltonian(): jnp.einsum('bxc,cd->bxd', block, yz_table, preferred_element_type=jnp.flo...  57.7 us
    dot_general x4, matrix products, hamiltonian(): jnp.einsum('bxc,cd->bxd', back, mag_yz, preferred_element_type=jnp.float32)  36.2 us
    dot_general x4, matrix products, hamiltonian(): jnp.einsum('ux,bxc->buc', mag_xt, weighted, preferred_element_type=jnp.fl...  31 us
    dot_general x4, matrix products, hamiltonian(): jnp.einsum('ux,bxc->buc', kin_x, block, preferred_element_type=jnp.float32)  28.2 us
    dot_general x8, matrix products, shards(): factor = 0.5 * (3.0 * eye - jnp.dot(iterate_z, iterate_a, precision=hp))  15.5 us
  transfers between devices with their start and end apart: 2, of which 2 were waited for; matrix products, arithmetic and copies ran while one was open for 0% of the time, Pallas kernels for 0%

commit v1 on v0

--- a/solution.py
+++ b/solution.py
@@ -83,7 +83,7 @@
         lax.dot_general(flat, flat, (((1,), (1,)), ((), ())), preferred_element_type=jnp.float32)
         * inverse_cells
     )
-    margin = lax.psum(partial_margin, "orb")
+    margin = jnp.sum(lax.all_gather(partial_margin, "orb"), axis=0)
     scale = jnp.sqrt(jnp.sum(margin * margin) + margin_eps)
     eye = jnp.eye(count_orb, dtype=jnp.float32)
     iterate_a = margin / scale

time: 575 us -> 660 us (1.15)
  waiting for transfers between devices: 200 us -> 278 us
    all_gather x0 -> x1, waiting for transfers between devices: none -> 188 us  [shards(): margin = jnp.sum(lax.all_gather(partial_margin, 'orb'), axis=0)]
    psum x1 -> x0, waiting for transfers between devices: 112 us -> none  [shards(): margin = lax.psum(partial_margin, 'orb')]
    reduce_sum x0 -> x1, other arithmetic: none -> 7.91 us  [shards(): margin = jnp.sum(lax.all_gather(partial_margin, 'orb'), axis=0)]
where the time goes in v1:
time: 660 us; the launch traced here: 652 us
  waiting for transfers between devices  278 us (42%)
  matrix products  203 us (31%)
  blocking collectives  103 us (16%)
  local copies, waits for them, and re-layouts  37.4 us (6%)
  between operations  15.3 us (2%)
  other arithmetic  8.79 us (1%)
  starting transfers between devices  7.63 us (1%)
    all_gather x1, waiting for transfers between devices, shards(): margin = jnp.sum(lax.all_gather(partial_margin, 'orb'), axis=0)  188 us
    all_to_all x1, blocking collectives, shards(): lax.all_to_all(filtered, 'orb', split_axis=2, concat_axis=1, tiled=True)  98.6 us
    all_to_all x1, waiting for transfers between devices, shards(): lax.all_to_all(rotated_cells, 'orb', split_axis=1, concat_axis=2, tiled=T...  89.4 us
    dot_general x4, matrix products, hamiltonian(): jnp.einsum('bxc,cd->bxd', block, yz_table, preferred_element_type=jnp.flo...  58 us
    dot_general x4, matrix products, hamiltonian(): jnp.einsum('bxc,cd->bxd', back, mag_yz, preferred_element_type=jnp.float32)  36 us
    dot_general x4, matrix products, hamiltonian(): jnp.einsum('ux,bxc->buc', mag_xt, weighted, preferred_element_type=jnp.fl...  31 us
    dot_general x4, matrix products, hamiltonian(): jnp.einsum('ux,bxc->buc', kin_x, block, preferred_element_type=jnp.float32)  28.3 us
    dot_general x8, matrix products, shards(): factor = 0.5 * (3.0 * eye - jnp.dot(iterate_z, iterate_a, precision=hp))  14.5 us
  transfers between devices with their start and end apart: 2, of which 2 were waited for; matrix products, arithmetic and copies ran while one was open for 0% of the time, Pallas kernels for 0%

profile of v1, /device:TPU:14, one launch (start us, length us, event | category | flops | bytes accessed | tf_op | source)
XLA Modules:
  0.0 652.4 jit_solution(12365948020558679456)
XLA Ops:
  7.2 0.0 copy-start.13
  7.2 0.0 copy-start.14
  7.2 0.0 all-gather.3.cloned.1.call-start
  7.2 15.1 %convolution_bitcast_fusion = f32[32,64,2048]{2,1,0:T(8,128)} fusion(bf16[1024,2048,1]{1,0,2:T(8,128)(2,1)} %constant.48, bf16[1,32,64,1024]{3,2,1,0:T(8,128)(2,1)} %param.7), kind=kOutput, calls=%fused_computation.39 | convolution fusion | flops 8589934592 | bytes 25165824 | tf_op jit(solution)/shard_map/bxc,cd->bxd/dot_general | solution.py:44
  22.4 7.7 %fusion.20 = bf16[32,1024,64]{1,2,0:T(8,128)(2,1)} fusion(bf16[64,64,1]{1,0,2:T(8,128)(2,1)S(1)} %copy-done.13, f32[64,1024]{1,0:T(8,128)S(1)} %copy-done.10, bf16[64,64,1]{1,0,2:T(8,128)(2,1)S(1)} %copy-done.14, f32[32,64,2048]{2,1,0:T(8,128)} %convolution_bitcast_fusion), kind=kOutput, calls=%fused_computation.41 | convolution fusion | flops 541065216 | bytes 8667136 | tf_op jit(solution)/shard_map/ux,bxc->buc/dot_general | solution.py:54
  30.1 7.1 %fusion.39 = f32[32,64,1024]{2,1,0:T(8,128)S(1)} fusion(bf16[1024,1024,1]{1,0,2:T(8,128)(2,1)} %constant.51, bf16[32,1024,64]{1,2,0:T(8,128)(2,1)} %fusion.20), kind=kOutput, calls=%fused_computation.56 | convolution fusion | flops 4294967296 | bytes 14680064 | tf_op jit(solution)/shard_map/bxc,cd->bxd/dot_general | solution.py:57
  37.2 5.4 fusion.2
  42.6 0.0 copy-start.3
  42.6 2.0 copy-done.3
  44.6 14.6 %fusion.65 = f32[32,64,2048]{2,1,0:T(8,128)} fusion(bf16[32,64,1024]{2,1,0:T(8,128)(2,1)S(1)} %fusion.2, bf16[1024,2048,1]{1,0,2:T(8,128)(2,1)} %constant.48), kind=kOutput, calls=%fused_computation.94 | convolution fusion | flops 8589934592 | bytes 25165824 | tf_op jit(solution)/shard_map/bxc,cd->bxd/dot_general | solution.py:44
  59.2 7.7 %fusion.22 = bf16[32,1024,64]{1,2,0:T(8,128)(2,1)} fusion(bf16[64,64,1]{1,0,2:T(8,128)(2,1)S(1)} %copy-done.13, f32[64,1024]{1,0:T(8,128)S(1)} %copy-done.10, bf16[64,64,1]{1,0,2:T(8,128)(2,1)S(1)} %copy-done.14, f32[32,64,2048]{2,1,0:T(8,128)} %fusion.65), kind=kOutput, calls=%fused_computation.42 | convolution fusion | flops 541065216 | bytes 8667136 | tf_op jit(solution)/shard_map/ux,bxc->buc/dot_general | solution.py:54
  66.8 10.7 %fusion.37 = f32[32,64,1024]{2,1,0:T(8,128)} fusion(bf16[1024,1024,1]{1,0,2:T(8,128)(2,1)} %constant.51, bf16[32,1024,64]{1,2,0:T(8,128)(2,1)} %fusion.22), kind=kOutput, calls=%fused_computation.54 | convolution fusion | flops 4294967296 | bytes 14680064 | tf_op jit(solution)/shard_map/bxc,cd->bxd/dot_general | solution.py:57
  77.6 7.6 %fusion.3 = bf16[32,64,1024]{2,1,0:T(8,128)(2,1)S(1)} fusion(bf16[32,64,1024]{2,1,0:T(8,128)(2,1)S(1)} %copy-done.4, f32[32,64,1024]{2,1,0:T(8,128)} %fusion.37, f32[32,64,2048]{2,1,0:T(8,128)} %fusion.65, bf16[1,32,64,1024]{3,2,1,0:T(8,128)(2,1)S(1)} %copy-done.9, bf16[64,64,1]{1,0,2:T(8,128)(2,1)S(1)} %copy-done.15), kind=kOutput, calls=%fused_computation.9 | convolution fusion | flops 287309824 | bytes 33570816 | tf_op jit(solution)/shard_map/ux,bxc->buc/dot_general | solution.py:47
  85.2 1.9 copy-done
  87.2 14.1 %fusion.66 = f32[32,64,2048]{2,1,0:T(8,128)} fusion(bf16[32,64,1024]{2,1,0:T(8,128)(2,1)S(1)} %fusion.3, bf16[1024,2048,1]{1,0,2:T(8,128)(2,1)} %constant.48), kind=kOutput, calls=%fused_computation.95 | convolution fusion | flops 8589934592 | bytes 25165824 | tf_op jit(solution)/shard_map/bxc,cd->bxd/dot_general | solution.py:44
  101.3 7.8 %fusion.24 = bf16[32,1024,64]{1,2,0:T(8,128)(2,1)} fusion(bf16[64,64,1]{1,0,2:T(8,128)(2,1)S(1)} %copy-done.13, f32[64,1024]{1,0:T(8,128)S(1)} %copy-done.10, bf16[64,64,1]{1,0,2:T(8,128)(2,1)S(1)} %copy-done.14, f32[32,64,2048]{2,1,0:T(8,128)} %fusion.66), kind=kOutput, calls=%fused_computation.43 | convolution fusion | flops 541065216 | bytes 8667136 | tf_op jit(solution)/shard_map/ux,bxc->buc/dot_general | solution.py:54
  109.1 9.1 %fusion.35 = f32[32,64,1024]{2,1,0:T(8,128)} fusion(bf16[1024,1024,1]{1,0,2:T(8,128)(2,1)S(1)} %copy-done.16, bf16[32,1024,64]{1,2,0:T(8,128)(2,1)} %fusion.24), kind=kOutput, calls=%fused_computation.52 | convolution fusion | flops 4294967296 | bytes 14680064 | tf_op jit(solution)/shard_map/bxc,cd->bxd/dot_general | solution.py:57
  118.2 7.6 %fusion.6 = bf16[32,64,1024]{2,1,0:T(8,128)(2,1)S(1)} fusion(bf16[32,64,1024]{2,1,0:T(8,128)(2,1)S(1)} %copy-done.5, bf16[32,64,1024]{2,1,0:T(8,128)(2,1)S(1)} %copy-done.1, f32[32,64,1024]{2,1,0:T(8,128)} %fusion.35, f32[32,64,2048]{2,1,0:T(8,128)} %fusion.66, bf16[64,64,1]{1,0,2:T(8,128)(2,1)S(1)} %copy-done.15), kind=kOutput, calls=%fused_computation.12 | convolution fusion | flops 287309824 | bytes 33570816 | tf_op jit(solution)/shard_map/ux,bxc->buc/dot_general | solution.py:47
  125.8 0.0 copy-start.6
  125.9 2.0 copy-done.6
  127.9 14.2 %fusion.67 = f32[32,64,2048]{2,1,0:T(8,128)} fusion(bf16[32,64,1024]{2,1,0:T(8,128)(2,1)S(1)} %fusion.6, bf16[1024,2048,1]{1,0,2:T(8,128)(2,1)} %constant.48), kind=kOutput, calls=%fused_computation.96 | convolution fusion | flops 8589934592 | bytes 25165824 | tf_op jit(solution)/shard_map/bxc,cd->bxd/dot_general | solution.py:44
  142.0 7.8 %fusion.26 = bf16[32,1024,64]{1,2,0:T(8,128)(2,1)} fusion(bf16[64,64,1]{1,0,2:T(8,128)(2,1)S(1)} %copy-done.13, f32[64,1024]{1,0:T(8,128)S(1)} %copy-done.10, bf16[64,64,1]{1,0,2:T(8,128)(2,1)S(1)} %copy-done.14, f32[32,64,2048]{2,1,0:T(8,128)} %fusion.67), kind=kOutput, calls=%fused_computation.44 | convolution fusion | flops 541065216 | bytes 8667136 | tf_op jit(solution)/shard_map/ux,bxc->buc/dot_general | solution.py:54
  149.8 9.1 %fusion.33 = f32[32,64,1024]{2,1,0:T(8,128)} fusion(bf16[1024,1024,1]{1,0,2:T(8,128)(2,1)S(1)} %copy-done.17, bf16[32,1024,64]{1,2,0:T(8,128)(2,1)} %fusion.26), kind=kOutput, calls=%fused_computation.50 | convolution fusion | flops 4294967296 | bytes 14680064 | tf_op jit(solution)/shard_map/bxc,cd->bxd/dot_general | solution.py:57
  158.9 7.6 %fusion.32 = bf16[1,32,64,1024]{3,2,1,0:T(8,128)(2,1)S(1)} fusion(bf16[32,64,1024]{2,1,0:T(8,128)(2,1)S(1)} %copy-done.2, bf16[32,64,1024]{2,1,0:T(8,128)(2,1)S(1)} %copy-done.7, f32[32,64,1024]{2,1,0:T(8,128)} %fusion.33, f32[32,64,2048]{2,1,0:T(8,128)} %fusion.67, bf16[64,64,1]{1,0,2:T(8,128)(2,1)S(1)} %copy-done.15), kind=kOutput, calls=%fused_computation.49 | convolution fusion | flops 287309824 | bytes 33570816 | tf_op jit(solution)/shard_map/ux,bxc->buc/dot_general | solution.py:47
  166.6 2.3 copy.16
  168.9 98.6 %all_to_all.33 = bf16[1,32,64,1024]{3,1,0,2:T(8,128)(2,1)S(1)} all-to-all(bf16[1,32,64,1024]{3,1,0,2:T(8,128)(2,1)S(1)} %copy.16), channel_id=1, replica_groups=mesh['kpt'=2,'orb'=16] {'orb'}, dimensions={2} | all-to-all | bytes 8388608 | tf_op jit(solution)/shard_map/all_to_all | solution.py:76
  267.5 3.5 copy.17
  271.1 2.3 copy.20
  273.4 2.0 copy-done.11
  275.4 3.3 convolution_multiply_fusion
  278.7 0.0 all-gather.3.cloned.1.call-update
  278.8 188.4 %all-gather.3.cloned.1.call-done = f32[8192,512]{1,0:T(8,128)} async-done(((f32[512,512]{1,0:T(8,128)}), f32[8192,512]{1,0:T(8,128)}) %all-gather.3.cloned.1.call-update) | async-done | bytes 16777232 | tf_op jit(solution)/shard_map/all_gather | solution.py:86
  467.1 7.9 %reduce_sum.27 = f32[512,512]{1,0:T(8,128)S(1)} reduce(f32[16,512,512]{2,1,0:T(8,128)} %bitcast.142, f32[]{:T(128)} %constant.28.clone.1), dimensions={0}, to_apply=%region_0.0 | reduce | flops 3932160 | bytes 17825796 | tf_op jit(solution)/shard_map/reduce_sum | solution.py:86
  475.0 0.9 multiply_reduce_fusion.1
  476.6 1.1 fusion.61
  477.7 2.1 fusion.64
  479.8 1.0 fusion.63
  480.8 1.9 fusion.54
  482.7 1.8 fusion.69
  484.5 1.8 fusion.68
  486.4 1.9 fusion.55
  488.2 1.8 fusion.71
  490.1 2.1 fusion.70
  492.2 1.8 fusion.56
  494.0 1.8 fusion.73
  495.9 1.8 fusion.72
  497.7 1.8 fusion.57
  499.6 1.8 fusion.75
  501.4 1.8 fusion.74
  503.3 2.3 fusion.58
  505.6 1.8 fusion.77
  507.4 1.8 fusion.76
  509.3 1.9 fusion.59
  511.1 1.8 fusion.78
  513.0 1.8 fusion.79
  514.9 1.9 fusion.60
  516.7 2.0 fusion.62
  518.8 4.4 multiply_reduce_fusion
  523.2 7.9 %reshape.13 = bf16[1,512,4,1024]{3,2,1,0:T(4,128)(2,1)} reshape(bf16[512,4096]{1,0:T(8,128)(2,1)} %get-tuple-element.3) | data formatting | bytes 8388608 | tf_op jit(solution)/shard_map/reshape | solution.py:99
  531.1 7.6 %all-to-all-start.1 = ((bf16[1,512,4,1024]{3,2,0,1:T(4,128)(2,1)}), bf16[1,512,4,1024]{3,2,0,1:T(4,128)(2,1)}, u32[]{:S(2)}, u32[]{:S(2)}) async-start(bf16[1,512,4,1024]{3,2,0,1:T(4,128)(2,1)} %bitcast.143), calls=%async_computation.1 | async-start | bytes 8388608 | tf_op jit(solution)/shard_map/all_to_all | solution.py:100
  538.7 4.0 psum.7
  542.6 89.4 %all-to-all-done.1 = bf16[1,512,4,1024]{3,2,0,1:T(4,128)(2,1)} async-done(((bf16[1,512,4,1024]{3,2,0,1:T(4,128)(2,1)}), bf16[1,512,4,1024]{3,2,0,1:T(4,128)(2,1)}, u32[]{:S(2)}, u32[]{:S(2)}) %all-to-all-start.1) | async-done | bytes 4194336 | tf_op jit(solution)/shard_map/all_to_all | solution.py:100
  632.1 6.4 copy.19
  638.5 6.9 %all_to_all.30 = bf16[1,32,64,1024]{3,2,1,0:T(8,128)(2,1)} reshape(bf16[1,32,16,4,1024]{4,3,2,1,0:T(4,128)(2,1)} %copy.19) | data formatting | bytes 8388608 | tf_op jit(solution)/shard_map/all_to_all | solution.py:100
  (30 shorter events, 0.1 us)
Async XLA Ops:
  7.2 15.2 %copy-start.13 = (bf16[64,64,1]{1,0,2:T(8,128)(2,1)S(1)}, bf16[64,64,1]{1,0,2:T(8,128)(2,1)}, u32[]{:S(2)}) copy-start(bf16[64,64,1]{1,0,2:T(8,128)(2,1)} %constant.50) | copy-start | bytes 24580
  7.2 15.2 %copy-start.14 = (bf16[64,64,1]{1,0,2:T(8,128)(2,1)S(1)}, bf16[64,64,1]{1,0,2:T(8,128)(2,1)}, u32[]{:S(2)}) copy-start(bf16[64,64,1]{1,0,2:T(8,128)(2,1)} %constant.49) | copy-start | bytes 24580
  7.2 15.2 %copy-start.10 = (f32[64,1024]{1,0:T(8,128)S(1)}, f32[64,1024]{1,0:T(8,128)}, u32[]{:S(2)}) copy-start(f32[64,1024]{1,0:T(8,128)} %param.8) | copy-start | bytes 786436
  7.2 459.9 %all-gather.3.cloned.1.call-start = ((), (), s32[]{:S(2)}) async-start(), calls=%async_computation.2 | async-start | bytes 17825792 | tf_op jit(solution)/shard_map/all_gather | solution.py:86
  30.1 7.1 %copy-start.8 = (bf16[1,32,64,1024]{3,2,1,0:T(8,128)(2,1)S(1)}, bf16[1,32,64,1024]{3,2,1,0:T(8,128)(2,1)}, u32[]{:S(2)}) copy-start(bf16[1,32,64,1024]{3,2,1,0:T(8,128)(2,1)} %param.7) | copy-start | bytes 12582916
  30.1 7.1 %copy-start.15 = (bf16[64,64,1]{1,0,2:T(8,128)(2,1)S(1)}, bf16[64,64,1]{1,0,2:T(8,128)(2,1)}, u32[]{:S(2)}) copy-start(bf16[64,64,1]{1,0,2:T(8,128)(2,1)} %constant.47) | copy-start | bytes 24580
  42.6 2.0 copy-start.3
  66.8 10.8 %copy-start.4 = (bf16[32,64,1024]{2,1,0:T(8,128)(2,1)S(1)}, bf16[32,64,1024]{2,1,0:T(8,128)(2,1)}, u32[]{:S(2)}) copy-start(bf16[32,64,1024]{2,1,0:T(8,128)(2,1)} %copy-done.3) | copy-start | bytes 12582916
  66.8 10.8 %copy-start.9 = (bf16[1,32,64,1024]{3,2,1,0:T(8,128)(2,1)S(1)}, bf16[1,32,64,1024]{3,2,1,0:T(8,128)(2,1)}, u32[]{:S(2)}) copy-start(bf16[1,32,64,1024]{3,2,1,0:T(8,128)(2,1)} %param.7) | copy-start | bytes 12582916
  85.2 2.0 copy-start
  101.3 7.8 %copy-start.16 = (bf16[1024,1024,1]{1,0,2:T(8,128)(2,1)S(1)}, bf16[1024,1024,1]{1,0,2:T(8,128)(2,1)}, u32[]{:S(2)}) copy-start(bf16[1024,1024,1]{1,0,2:T(8,128)(2,1)} %constant.51) | copy-start | bytes 6291460
  109.1 9.1 %copy-start.1 = (bf16[32,64,1024]{2,1,0:T(8,128)(2,1)S(1)}, bf16[32,64,1024]{2,1,0:T(8,128)(2,1)}, u32[]{:S(2)}) copy-start(bf16[32,64,1024]{2,1,0:T(8,128)(2,1)} %copy-done) | copy-start | bytes 12582916
  109.1 9.1 %copy-start.5 = (bf16[32,64,1024]{2,1,0:T(8,128)(2,1)S(1)}, bf16[32,64,1024]{2,1,0:T(8,128)(2,1)}, u32[]{:S(2)}) copy-start(bf16[32,64,1024]{2,1,0:T(8,128)(2,1)} %copy-done.3) | copy-start | bytes 12582916
  125.8 2.0 copy-start.6
  142.0 7.8 %copy-start.17 = (bf16[1024,1024,1]{1,0,2:T(8,128)(2,1)S(1)}, bf16[1024,1024,1]{1,0,2:T(8,128)(2,1)}, u32[]{:S(2)}) copy-start(bf16[1024,1024,1]{1,0,2:T(8,128)(2,1)} %constant.51) | copy-start | bytes 6291460
  149.8 9.1 %copy-start.2 = (bf16[32,64,1024]{2,1,0:T(8,128)(2,1)S(1)}, bf16[32,64,1024]{2,1,0:T(8,128)(2,1)}, u32[]{:S(2)}) copy-start(bf16[32,64,1024]{2,1,0:T(8,128)(2,1)} %copy-done) | copy-start | bytes 12582916
  149.8 9.1 %copy-start.7 = (bf16[32,64,1024]{2,1,0:T(8,128)(2,1)S(1)}, bf16[32,64,1024]{2,1,0:T(8,128)(2,1)}, u32[]{:S(2)}) copy-start(bf16[32,64,1024]{2,1,0:T(8,128)(2,1)} %copy-done.6) | copy-start | bytes 12582916
  273.4 2.0 copy-start.11
  514.9 3.9 copy-start.12
  531.1 101.0 %all-to-all-start.1 = ((bf16[1,512,4,1024]{3,2,0,1:T(4,128)(2,1)}), bf16[1,512,4,1024]{3,2,0,1:T(4,128)(2,1)}, u32[]{:S(2)}, u32[]{:S(2)}) async-start(bf16[1,512,4,1024]{3,2,0,1:T(4,128)(2,1)} %bitcast.143), calls=%async_computation.1 | async-start | bytes 8388608 | tf_op jit(solution)/shard_map/all_to_all | solution.py:100
Sparse Core Ops, SparseCore 0:
  278.9 188.1 all-gather.2
